TPU v7x, 32 devices: a whole 2x2x4 slice. The times are simulated.
32 devices in a mesh: sx: 4 (over z), sy: 8 (over y, x, core).
Axes of the slice: x: 2, y: 2, z: 4, core: 2. Of those that a mesh axis runs over, the one named last changes fastest.
Arguments:
- residual: bfloat16 [4, 8, 2048, 128], P('sx', 'sy'), may hold values from -6 to 6
- weights: float32 [4, 8, 2048], P('sx', 'sy'), may hold values from 0.1 to 1.9
- blocks: bfloat16 [4, 8, 16, 4, 128, 128], P('sx', 'sy'), may hold values from -0.25 to 0.25
- pattern: int32 [4, 8, 16, 4], P('sx', 'sy'), may hold values from 0 to 15
- primal_basis: bfloat16 [4, 8, 2048, 64], P('sx', 'sy'), may hold values from -0.25 to 0.25
- coarse_inverse: float32 [4, 512, 512], P('sx', 'sy'), may hold values from -0.25 to 0.25
- coarse_rows: int32 [4, 512], P('sx'), may hold values from 0 to 511, each once within a row
- shared_lists: int32 [4, 8, 4, 512], P('sx', 'sy'), may hold values from 0 to 511, each once within a row
Outputs:
- preconditioned: bfloat16 [4, 8, 2048, 128], P('sx', 'sy')
Inputs may be any that keep to these rules, and one draw needn't show every extreme that they name: `pattern`: block column indices; one block row may name a column twice. `coarse_rows`: each row of a grid row's map names every coarse row once. `shared_lists`: each face's list names every row of the face once.
All inputs are finite; a program needn't handle non-finite values.
Results may differ from a plain program's by a relative error of at most 0.0085.
Values may be sent and summed in bfloat16 or wider, within the bound.
A program may use at most 64 MiB of HBM per device.

v0:
```python
import jax
import jax.numpy as jnp
from jax import lax
from jax.sharding import PartitionSpec as P


def with_halo(block, sides, width):
    for axis, dim in sides:
        count = lax.axis_size(axis)
        forward = [(i, i + 1) for i in range(count - 1)]
        backward = [(target, source) for source, target in forward]
        low = lax.ppermute(
            lax.slice_in_dim(block, block.shape[dim] - width, None, axis=dim), axis, forward
        )
        high = lax.ppermute(lax.slice_in_dim(block, 0, width, axis=dim), axis, backward)
        block = jnp.concatenate([low, block, high], axis=dim)
    return block


def add_across(faces, padded_rows, padded_cols, shared):
    north = padded_rows[0, 0][shared[0]]
    south = padded_rows[3, 0][shared[1]]
    west = padded_cols[0, 0][shared[2]]
    east = padded_cols[0, 3][shared[3]]
    return faces + jnp.stack([north, south, west, east])


def body(
    residual, weights, blocks, pattern, primal_basis, coarse_inverse, coarse_rows, shared_lists
):
    nvec = residual.shape[-1]
    ninter = residual.shape[-2]
    nblocks, knz, blk = (blocks.shape[2], blocks.shape[3], blocks.shape[4])
    nprim = primal_basis.shape[-1]
    face = shared_lists.shape[-1]
    scale = weights[0, 0][:, None]
    shared = shared_lists[0, 0]
    basis = primal_basis[0, 0]
    weighted = (scale * residual[0, 0].astype(jnp.float32)).astype(jnp.bfloat16)
    pieces = weighted.reshape(nblocks, blk, nvec)[pattern[0, 0]]
    solved = jnp.einsum(
        "bkrc,bkcn->brn", blocks[0, 0], pieces, preferred_element_type=jnp.float32
    ).reshape(ninter, nvec)
    primal_vals = jnp.einsum("ip,in->pn", basis, weighted, preferred_element_type=jnp.float32)
    gathered = lax.all_gather(primal_vals, "sy", axis=0, tiled=True)
    order = coarse_rows[0]
    coarse_rhs = jnp.zeros_like(gathered).at[order].set(gathered)
    own_rows = jnp.dot(coarse_inverse[0], coarse_rhs, precision=lax.Precision.HIGHEST)
    coarse_sol = lax.all_gather(own_rows.astype(jnp.bfloat16), "sy", axis=0, tiled=True).astype(
        own_rows.dtype
    )
    start = lax.axis_index("sy") * nprim
    own_order = lax.dynamic_slice_in_dim(order, start, nprim)
    primal_sol = coarse_sol[own_order].astype(jnp.bfloat16)
    correction = jnp.dot(basis, primal_sol, preferred_element_type=jnp.float32)
    value = (scale * (solved + correction)).reshape(4, face, nvec)
    padded_rows = with_halo(value[0:2][:, None], (("sx", 0),), 1)
    padded_cols = with_halo(value[2:4][None], (("sy", 1),), 1)
    total = add_across(value, padded_rows, padded_cols, shared)
    return total.reshape(1, 1, ninter, nvec).astype(jnp.bfloat16)


def solution(mesh):
    return jax.shard_map(
        body,
        mesh=mesh,
        in_specs=(
            P("sx", "sy", None, None),
            P("sx", "sy", None),
            P("sx", "sy", None, None, None, None),
            P("sx", "sy", None, None),
            P("sx", "sy", None, None),
            P("sx", "sy", None),
            P("sx", None),
            P("sx", "sy", None, None),
        ),
        out_specs=P("sx", "sy", None, None),
        check_vma=False,
    )
```

profile of v0, /device:TPU:0, one launch (start us, length us, event | category | flops | bytes accessed | tf_op | source)
XLA Modules:
  0.0 71.1 jit_solution(18182687352474169073)
XLA Ops:
  0.0 0.8 %compare_select_fusion.5 = s32[16,4,1]{0,1,2:T(4,128)S(1)} fusion(s32[1,1,16,4]{2,3,1,0:T(4,128)} %param.11), kind=kLoop, calls=%fused_computation.36 | loop fusion | flops 192 | bytes 512 | tf_op jit(solution)/shard_map/select_n | solution.py:40
  1.0 1.4 %multiply_convert_fusion.1 = bf16[16,128,128]{2,1,0:T(8,128)(2,1)S(1)} fusion(f32[16,128]{1,0:T(8,128)} %bitcast.90, bf16[16,128,128]{2,1,0:T(8,128)(2,1)} %bitcast.87), kind=kLoop, calls=%fused_computation.18 | loop fusion | flops 786432 | bytes 1056768 | tf_op jit(solution)/shard_map/convert_element_type | solution.py:39
  2.4 2.2 %gather_fusion = bf16[64,128,128]{2,1,0:T(8,128)(2,1)} fusion(bf16[16,128,128]{2,1,0:T(8,128)(2,1)S(1)} %multiply_convert_fusion.1, s32[1024]{0:T(1024)S(1)} %pad_clamp_fusion.5), kind=kCustom, calls=%fused_computation | custom fusion | bytes 4194560 | tf_op jit(solution)/shard_map/gather | solution.py:40
  4.6 2.3 %fusion.2 = f32[16,128,128,1]{1,2,3,0:T(8,128)S(1)} fusion(bf16[16,4,128,128]{3,2,1,0:T(8,128)(2,1)} %bitcast.79, bf16[1,1,16,4,128,128]{5,4,3,2,1,0:T(8,128)(2,1)S(1)} %copy-done), kind=kOutput, calls=%fused_computation.10 | convolution fusion | flops 268435456 | bytes 5242880 | tf_op jit(solution)/shard_map/bkrc,bkcn->brn/dot_general | solution.py:41
  6.9 1.3 %copy.18 = f32[2048,128]{0,1:T(8,128)} copy(f32[2048,128]{1,0:T(8,128)S(1)} %bitcast.80) | data formatting | bytes 2097152 | tf_op jit(solution)/shard_map/reshape | solution.py:43
  8.3 1.6 %convolution_bitcast_fusion.1 = f32[64,128]{1,0:T(8,128)S(1)} fusion(f32[2048]{0:T(1024)S(1)} %bitcast.91, bf16[1,1,2048,64]{2,3,1,0:T(8,128)(2,1)S(1)} %copy-done.4, bf16[1,1,2048,128]{3,2,1,0:T(8,128)(2,1)} %param.8), kind=kOutput, calls=%fused_computation.12 | convolution fusion | flops 34340864 | bytes 827392 | tf_op jit(solution)/shard_map/ip,in->pn/dot_general | solution.py:44
  9.9 11.8 %all_gather.6 = f32[512,128]{1,0:T(8,128)} all-gather(f32[64,128]{1,0:T(8,128)S(1)} %convolution_bitcast_fusion.1), channel_id=1, replica_groups=mesh['sx'=4,'sy'=8] {'sy'}, dimensions={0}, use_global_device_ids=true | all-gather | bytes 294912 | tf_op jit(solution)/shard_map/all_gather | solution.py:45
  21.7 2.2 %scatter_custom_fusion = f32[512,128]{1,0:T(8,128)S(1)} fusion(s32[512]{0:T(512)S(1)} %bitcast.97, f32[512,128]{1,0:T(8,128)} %all_gather.6, f32[]{:T(128)} %constant.8.clone.1), kind=kCustom, calls=%fused_computation.28 | custom fusion | bytes 262656 | tf_op jit(solution)/shard_map/scatter | solution.py:47
  23.9 0.3 fusion.4
  24.2 9.1 %all_gather.7 = bf16[512,128]{1,0:T(8,128)(2,1)S(1)} all-gather(bf16[64,128]{1,0:T(8,128)(2,1)S(1)} %fusion.4), channel_id=1, replica_groups=mesh['sx'=4,'sy'=8] {'sy'}, dimensions={0}, use_global_device_ids=true | all-gather | bytes 147456 | tf_op jit(solution)/shard_map/all_gather | solution.py:49
  33.4 0.6 gather_fusion.1
  34.0 1.3 %fusion.1 = f32[2048,128]{0,1:T(8,128)S(1)} fusion(f32[2048,128]{0,1:T(8,128)S(1)} %copy-done.3, f32[2048]{0:T(1024)S(1)} %bitcast.92, bf16[1,1,2048,64]{2,3,1,0:T(8,128)(2,1)} %param.12, bf16[64,128]{1,0:T(8,128)(2,1)S(1)} %gather_fusion.1), kind=kOutput, calls=%fused_computation.9 | convolution fusion | flops 34078720 | bytes 2383872 | tf_op jit(solution)/shard_map/dot_general | solution.py:55
  35.3 1.0 %copy-done.1 = f32[2048,128]{0,1:T(8,128)} copy-done((f32[2048,128]{0,1:T(8,128)}, f32[2048,128]{0,1:T(8,128)S(1)}, u32[]{:S(2)}) %copy-start.1) | copy-done | bytes 1048600
  36.4 0.2 copy.27
  36.6 0.8 %fusion.17 = (f32[1,1,512,128]{3,2,1,0:T(8,128)}, f32[1,1,512,128]{3,2,1,0:T(8,128)}) fusion(f32[1,2,512,128]{3,2,1,0:T(8,128)S(1)} %bitcast.82), kind=kLoop, calls=%fused_computation.45 | loop fusion | bytes 1048576 | tf_op jit(solution)/shard_map/slice | solution.py:13
  37.4 1.3 %collective-permute-start.3 = (f32[1,1,512,128]{3,2,1,0:T(8,128)}, f32[1,1,512,128]{3,2,1,0:T(8,128)S(1)}, u32[]{:S(2)}, u32[]{:S(2)}) collective-permute-start(f32[1,1,512,128]{3,2,1,0:T(8,128)} %get-tuple-element.8), channel_id=1, source_target_pairs={{1,0},{2,1},{3,2},{4,3},{5,4},{6,5},{7,6},{9,8},{10,9},{11,10},{12... | collective-permute-start | bytes 786440 | tf_op jit(solution)/shard_map/ppermute | solution.py:15
  38.7 3.0 %collective-permute-start.2 = (f32[1,1,512,128]{3,2,1,0:T(8,128)}, f32[1,1,512,128]{3,2,1,0:T(8,128)S(1)}, u32[]{:S(2)}, u32[]{:S(2)}) collective-permute-start(f32[1,1,512,128]{3,2,1,0:T(8,128)} %get-tuple-element.7), channel_id=1, source_target_pairs={{0,1},{1,2},{2,3},{3,4},{4,5},{5,6},{6,7},{8,9},{9,10},{10,11},{11... | collective-permute-start | bytes 786440 | tf_op jit(solution)/shard_map/ppermute | solution.py:12
  41.7 1.8 %slice_bitcast_fusion.1 = (f32[1,1,512,128]{2,3,1,0:T(8,128)}, f32[1,1,512,128]{2,3,1,0:T(8,128)S(1)}) fusion(f32[2048,128]{0,1:T(8,128)} %copy-done.1), kind=kLoop, calls=%fused_computation.23 | loop fusion | bytes 1048576 | tf_op jit(solution)/shard_map/slice | solution.py:13
  43.5 1.3 %collective-permute-start.1 = (f32[1,1,512,128]{2,3,1,0:T(8,128)S(1)}, f32[1,1,512,128]{2,3,1,0:T(8,128)S(1)}, u32[]{:S(2)}, u32[]{:S(2)}) collective-permute-start(f32[1,1,512,128]{2,3,1,0:T(8,128)S(1)} %get-tuple-element.6), channel_id=1, source_target_pairs={{8,0},{16,8},{24,16},{9,1},{17,9},{25,17},{10,2},{18,10},{26,18},{... | collective-permute-start | bytes 786440 | tf_op jit(solution)/shard_map/ppermute | solution.py:15
  44.8 4.6 %collective-permute-start = (f32[1,1,512,128]{2,3,1,0:T(8,128)}, f32[1,1,512,128]{2,3,1,0:T(8,128)S(1)}, u32[]{:S(2)}, u32[]{:S(2)}) collective-permute-start(f32[1,1,512,128]{2,3,1,0:T(8,128)} %get-tuple-element.5), channel_id=1, source_target_pairs={{0,8},{8,16},{16,24},{1,9},{9,17},{17,25},{2,10},{10,18},{18,26},{... | collective-permute-start | bytes 786440 | tf_op jit(solution)/shard_map/ppermute | solution.py:12
  49.5 4.6 %collective-permute-done.1 = f32[1,1,512,128]{2,3,1,0:T(8,128)S(1)} collective-permute-done((f32[1,1,512,128]{2,3,1,0:T(8,128)S(1)}, f32[1,1,512,128]{2,3,1,0:T(8,128)S(1)}, u32[]{:S(2)}, u32[]{:S(2)}) %collective-permute-start.1) | collective-permute-done | bytes 262176 | tf_op jit(solution)/shard_map/ppermute | solution.py:15
  54.1 0.1 copy.20
  54.2 1.9 %collective-permute-done = f32[1,1,512,128]{2,3,1,0:T(8,128)S(1)} collective-permute-done((f32[1,1,512,128]{2,3,1,0:T(8,128)}, f32[1,1,512,128]{2,3,1,0:T(8,128)S(1)}, u32[]{:S(2)}, u32[]{:S(2)}) %collective-permute-start) | collective-permute-done | bytes 262176 | tf_op jit(solution)/shard_map/ppermute | solution.py:12
  56.1 0.1 copy.19
  56.2 1.0 %gather_fusion.5 = f32[512,128]{1,0:T(8,128)S(1)} fusion(f32[512,128]{1,0:T(8,128)S(1)} %bitcast.78, s32[1024]{0:T(1024)S(1)} %pad_clamp_fusion), kind=kCustom, calls=%fused_computation.5 | custom fusion | bytes 526336 | tf_op jit(solution)/shard_map/gather | solution.py:24
  57.2 1.6 %gather_fusion.4 = f32[512,128]{1,0:T(8,128)} fusion(f32[512,128]{1,0:T(8,128)S(1)} %bitcast.77, s32[1024]{0:T(1024)S(1)} %pad_clamp_fusion.1), kind=kCustom, calls=%fused_computation.4 | custom fusion | bytes 526336 | tf_op jit(solution)/shard_map/gather | solution.py:23
  58.9 1.6 %gather_fusion.3 = f32[512,128]{1,0:T(8,128)} fusion(f32[512,128]{1,0:T(8,128)S(1)} %copy.20, s32[1024]{0:T(1024)S(1)} %pad_clamp_fusion.2), kind=kCustom, calls=%fused_computation.3 | custom fusion | bytes 526336 | tf_op jit(solution)/shard_map/gather | solution.py:22
  60.5 1.6 %gather_fusion.2 = f32[512,128]{1,0:T(8,128)} fusion(f32[512,128]{1,0:T(8,128)S(1)} %copy.19, s32[1024]{0:T(1024)S(1)} %pad_clamp_fusion.3), kind=kCustom, calls=%fused_computation.2 | custom fusion | bytes 526336 | tf_op jit(solution)/shard_map/gather | solution.py:21
  62.2 2.3 %pad_maximum_fusion = f32[4,512,128]{2,1,0:T(8,128)} fusion(f32[1,512,128]{2,1,0:T(8,128)S(1)} %bitcast.83, f32[1,512,128]{2,1,0:T(8,128)} %bitcast.84, f32[1,512,128]{2,1,0:T(8,128)} %bitcast.85, f32[1,512,128]{2,1,0:T(8,128)} %bitcast.86), kind=kLoop, calls=%fused_computation.15 | loop fusion | flops 786432 | bytes 2097152 | tf_op jit(solution)/shard_map/stack | solution.py:25
  64.5 2.5 %copy.26 = f32[2048,128]{0,1:T(8,128)} copy(f32[2048,128]{1,0:T(8,128)} %bitcast.81) | data formatting | bytes 2097152 | tf_op jit(solution)/shard_map/stack | solution.py:25
  67.0 2.1 %fusion.7 = bf16[1,1,2048,128]{2,3,1,0:T(8,128)(2,1)} fusion(f32[2048,128]{0,1:T(8,128)S(1)} %copy-done.2, f32[2048,128]{0,1:T(8,128)} %copy.26), kind=kLoop, calls=%fused_computation.20 | loop fusion | flops 524288 | bytes 2621440 | tf_op jit(solution)/shard_map/convert_element_type | solution.py:60
  69.1 2.0 %copy.24 = bf16[1,1,2048,128]{3,2,1,0:T(8,128)(2,1)} copy(bf16[1,1,2048,128]{2,3,1,0:T(8,128)(2,1)} %fusion.7) | data formatting | bytes 1048576 | tf_op jit(solution)/shard_map/convert_element_type | solution.py:60
  (31 shorter events, 0.4 us)
Async XLA Ops:
  0.0 4.6 %copy-start = (bf16[1,1,16,4,128,128]{5,4,3,2,1,0:T(8,128)(2,1)S(1)}, bf16[1,1,16,4,128,128]{5,4,3,2,1,0:T(8,128)(2,1)}, u32[]{:S(2)}) copy-start(bf16[1,1,16,4,128,128]{5,4,3,2,1,0:T(8,128)(2,1)} %param.10) | copy-start | bytes 6291460
  6.9 1.4 %copy-start.8 = (s32[1,512]{1,0:T(1,128)S(1)}, s32[1,512]{1,0:T(1,128)}, u32[]{:S(2)}) copy-start(s32[1,512]{1,0:T(1,128)} %param.14) | copy-start | bytes 6148
  6.9 1.4 %copy-start.4 = (bf16[1,1,2048,64]{2,3,1,0:T(8,128)(2,1)S(1)}, bf16[1,1,2048,64]{2,3,1,0:T(8,128)(2,1)}, u32[]{:S(2)}) copy-start(bf16[1,1,2048,64]{2,3,1,0:T(8,128)(2,1)} %param.12) | copy-start | bytes 786436
  6.9 1.4 %copy-start.6 = (f32[1,1,2048]{2,1,0:T(1,128)S(1)}, f32[1,1,2048]{2,1,0:T(1,128)}, u32[]{:S(2)}) copy-start(f32[1,1,2048]{2,1,0:T(1,128)} %param.9) | copy-start | bytes 24580
  6.9 17.0 %copy-start.5 = (f32[1,64,512]{2,1,0:T(8,128)S(1)}, f32[1,64,512]{2,1,0:T(8,128)}, u32[]{:S(2)}) copy-start(f32[1,64,512]{2,1,0:T(8,128)} %param.13) | copy-start | bytes 393220
  8.2 25.8 %copy-start.3 = (f32[2048,128]{0,1:T(8,128)S(1)}, f32[2048,128]{0,1:T(8,128)}, u32[]{:S(2)}) copy-start(f32[2048,128]{0,1:T(8,128)} %copy.18) | copy-start | bytes 3145732
  35.3 1.0 %copy-start.1 = (f32[2048,128]{0,1:T(8,128)}, f32[2048,128]{0,1:T(8,128)S(1)}, u32[]{:S(2)}) copy-start(f32[2048,128]{0,1:T(8,128)S(1)} %fusion.1) | copy-start | bytes 3145732
  36.3 13.1 %copy-start.7 = (s32[1,1,4,512]{3,2,1,0:T(4,128)S(1)}, s32[1,1,4,512]{3,2,1,0:T(4,128)}, u32[]{:S(2)}) copy-start(s32[1,1,4,512]{3,2,1,0:T(4,128)} %param.15) | copy-start | bytes 24580
  37.4 18.8 %collective-permute-start.3 = (f32[1,1,512,128]{3,2,1,0:T(8,128)}, f32[1,1,512,128]{3,2,1,0:T(8,128)S(1)}, u32[]{:S(2)}, u32[]{:S(2)}) collective-permute-start(f32[1,1,512,128]{3,2,1,0:T(8,128)} %get-tuple-element.8), channel_id=1, source_target_pairs={{1,0},{2,1},{3,2},{4,3},{5,4},{6,5},{7,6},{9,8},{10,9},{11,10},{12... | collective-permute-start | bytes 786440 | tf_op jit(solution)/shard_map/ppermute | solution.py:15
  38.7 18.5 %collective-permute-start.2 = (f32[1,1,512,128]{3,2,1,0:T(8,128)}, f32[1,1,512,128]{3,2,1,0:T(8,128)S(1)}, u32[]{:S(2)}, u32[]{:S(2)}) collective-permute-start(f32[1,1,512,128]{3,2,1,0:T(8,128)} %get-tuple-element.7), channel_id=1, source_target_pairs={{0,1},{1,2},{2,3},{3,4},{4,5},{5,6},{6,7},{8,9},{9,10},{10,11},{11... | collective-permute-start | bytes 786440 | tf_op jit(solution)/shard_map/ppermute | solution.py:12
  43.5 10.5 %collective-permute-start.1 = (f32[1,1,512,128]{2,3,1,0:T(8,128)S(1)}, f32[1,1,512,128]{2,3,1,0:T(8,128)S(1)}, u32[]{:S(2)}, u32[]{:S(2)}) collective-permute-start(f32[1,1,512,128]{2,3,1,0:T(8,128)S(1)} %get-tuple-element.6), channel_id=1, source_target_pairs={{8,0},{16,8},{24,16},{9,1},{17,9},{25,17},{10,2},{18,10},{26,18},{... | collective-permute-start | bytes 786440 | tf_op jit(solution)/shard_map/ppermute | solution.py:15
  44.8 11.2 %collective-permute-start = (f32[1,1,512,128]{2,3,1,0:T(8,128)}, f32[1,1,512,128]{2,3,1,0:T(8,128)S(1)}, u32[]{:S(2)}, u32[]{:S(2)}) collective-permute-start(f32[1,1,512,128]{2,3,1,0:T(8,128)} %get-tuple-element.5), channel_id=1, source_target_pairs={{0,8},{8,16},{16,24},{1,9},{9,17},{17,25},{2,10},{10,18},{18,26},{... | collective-permute-start | bytes 786440 | tf_op jit(solution)/shard_map/ppermute | solution.py:12
  62.2 4.8 %copy-start.2 = (f32[2048,128]{0,1:T(8,128)S(1)}, f32[2048,128]{0,1:T(8,128)}, u32[]{:S(2)}) copy-start(f32[2048,128]{0,1:T(8,128)} %copy-done.1) | copy-start | bytes 3145732
where the time goes:
time: 71.7 us; the launch traced here: 71.1 us
  local copies, waits for them, and re-layouts  21.1 us (29%)
  blocking collectives  20.9 us (29%)
  starting transfers between devices  10.2 us (14%)
  other arithmetic  6.74 us (9%)
  waiting for transfers between devices  6.46 us (9%)
  matrix products  5.47 us (8%)
    all_gather x1, blocking collectives, body(): gathered = lax.all_gather(primal_vals, 'sy', axis=0, tiled=True)  11.8 us
    all_gather x1, blocking collectives, body(): lax.all_gather(own_rows.astype(jnp.bfloat16), 'sy', axis=0, tiled=True)  9.13 us
    ppermute x2, starting transfers between devices, with_halo(): lax.ppermute(lax.slice_in_dim(block, block.shape[dim] - width, None, axis...  7.61 us
    ppermute x2, waiting for transfers between devices, with_halo(): lax.ppermute(lax.slice_in_dim(block, 0, width, axis=dim), axis, backward)  4.59 us
    slice x2, local copies, waits for them, and re-layouts, with_halo(): lax.slice_in_dim(block, block.shape[dim] - width, None, axis=dim)  2.63 us
    ppermute x2, starting transfers between devices, with_halo(): lax.ppermute(lax.slice_in_dim(block, 0, width, axis=dim), axis, backward)  2.56 us
    another operation x1, local copies, waits for them, and re-layouts, add_across(): return faces + jnp.stack([north, south, west, east])  2.53 us
    dot_general x1, matrix products, body(): jnp.einsum('bkrc,bkcn->brn', blocks[0, 0], pieces, preferred_element_type...  2.28 us
  transfers between devices with their start and end apart: 4, of which 2 were waited for; matrix products, arithmetic and copies ran while one was open for 4% of the time, Pallas kernels for 0%

commit v1 on v0

v1 whole, which is shorter than its diff:
```python
import functools

import jax
import jax.numpy as jnp
from jax import lax
from jax.experimental import pallas as pl
from jax.experimental.pallas import tpu as pltpu
from jax.sharding import PartitionSpec as P

MESH = pl.DeviceIdType.MESH
F32 = jnp.float32
BF16 = jnp.bfloat16
LANES = 128
OPPOSITE = (1, 0, 3, 2)


def down_rows(row):
    return jnp.broadcast_to(row, (LANES, LANES)).T


def kernel(
    n_sx, n_sy,
    res_hbm, w_ref, blocks_hbm, pat_ref, basis_hbm, inv_hbm, ord_ref, sh_ref,
    out_hbm,
    res, basis, blocks, inv, wcol, weighted, acc, comb, onehot, inv_perm, pick, cols,
    gath, csol, psol, face_out, basis_out, face_in, basis_in, psol_in, out,
    in_sem, blk_sem, out_sem, pv_s, pv_r, cs_s, cs_r, fb_s, fb_r, fw_s, fw_r, ps_s, ps_r,
):
    i, j = lax.axis_index("sx"), lax.axis_index("sy")
    nb, knz, blk, _ = blocks.shape
    nprim, ncr = inv.shape
    ni, nvec = res.shape
    face = ni // 4
    per = face // blk

    load_basis = pltpu.make_async_copy(basis_hbm, basis, in_sem.at[0])
    load_res = pltpu.make_async_copy(res_hbm, res, in_sem.at[1])
    load_inv = pltpu.make_async_copy(inv_hbm, inv, in_sem.at[2])
    load_blocks = [
        pltpu.make_async_copy(
            blocks_hbm.at[pl.ds(f * per, per)], blocks.at[pl.ds(f * per, per)], blk_sem.at[f]
        )
        for f in range(4)
    ]
    load_basis.start()
    load_res.start()
    load_inv.start()
    for copy in load_blocks:
        copy.start()

    has = (i > 0, i < n_sx - 1, j > 0, j < n_sy - 1)
    there = ((i - 1, j), (i + 1, j), (i, j - 1), (i, j + 1))

    barrier = pltpu.get_barrier_semaphore()

    def greet(step, carry):
        peer = lax.rem(j + step, n_sy)
        pl.semaphore_signal(barrier, inc=1, device_id=(i, peer), device_id_type=MESH)
        return carry

    lax.fori_loop(1, n_sy, greet, 0)
    for f in (0, 1):

        @pl.when(has[f])
        def _():
            pl.semaphore_signal(barrier, inc=1, device_id=there[f], device_id_type=MESH)

    def basis_copy(f):
        return pltpu.make_async_remote_copy(
            src_ref=basis_out.at[f], dst_ref=basis_in.at[OPPOSITE[f]],
            send_sem=fb_s.at[f], recv_sem=fb_r.at[OPPOSITE[f]],
            device_id=there[f], device_id_type=MESH,
        )

    def face_copy(f):
        return pltpu.make_async_remote_copy(
            src_ref=face_out.at[f], dst_ref=face_in.at[OPPOSITE[f]],
            send_sem=fw_s.at[f], recv_sem=fw_r.at[OPPOSITE[f]],
            device_id=there[f], device_id_type=MESH,
        )

    def psol_copy(f):
        return pltpu.make_async_remote_copy(
            src_ref=psol.at[0], dst_ref=psol_in.at[OPPOSITE[f]],
            send_sem=ps_s.at[f], recv_sem=ps_r.at[OPPOSITE[f]],
            device_id=there[f], device_id_type=MESH,
        )

    def rows_copy(buf, send, recv, peer, slot):
        rows = pl.ds(pl.multiple_of(slot * nprim, nprim), nprim)
        return pltpu.make_async_remote_copy(
            src_ref=buf.at[rows], dst_ref=buf.at[rows],
            send_sem=send.at[peer], recv_sem=recv.at[slot],
            device_id=(i, peer), device_id_type=MESH,
        )

    def send_rows(buf, send, recv):
        def step(d, carry):
            rows_copy(buf, send, recv, lax.rem(j + d, n_sy), j).start()
            return carry

        lax.fori_loop(1, n_sy, step, 0)

    def wait_rows(buf, send, recv):
        def step(d, carry):
            peer = lax.rem(j + d, n_sy)
            rows_copy(buf, send, recv, peer, peer).wait_recv()
            return carry

        lax.fori_loop(1, n_sy, step, 0)

    def drain_rows(buf, send, recv):
        def step(d, carry):
            rows_copy(buf, send, recv, lax.rem(j + d, n_sy), j).wait_send()
            return carry

        lax.fori_loop(1, n_sy, step, 0)

    for f in range(4):

        @pl.when(jnp.logical_not(has[f]))
        def _():
            face_in[f] = jnp.zeros(face_in.shape[1:], BF16)
            basis_in[f] = jnp.zeros(basis_in.shape[1:], BF16)
            if f < 2:
                psol_in[f] = jnp.zeros(psol_in.shape[1:], BF16)

    for b in range(nb):
        wcol[b] = down_rows(w_ref[0:1, b * blk : (b + 1) * blk])
    load_basis.wait()
    load_res.wait()
    for b in range(nb):
        rows = slice(b * blk, (b + 1) * blk)
        weighted[b] = (wcol[b] * res[rows, :].astype(F32)).astype(BF16)
    pv = lax.dot_general(
        basis[...], weighted[...].reshape(ni, nvec), (((0,), (0,)), ((), ())),
        preferred_element_type=F32,
    )
    own = pl.ds(pl.multiple_of(j * nprim, nprim), nprim)
    gath[own, :] = pv.astype(BF16)

    pl.semaphore_wait(
        barrier, n_sy - 1 + has[0].astype(jnp.int32) + has[1].astype(jnp.int32)
    )
    send_rows(gath, pv_s, pv_r)

    half = per // 2
    for f in range(4):
        parts = []
        for b in range(f * per, (f + 1) * per):
            rows = slice(b * blk, (b + 1) * blk)
            parts.append(wcol[b][:, :nprim] * basis[rows, :].astype(F32))
        zero = jnp.zeros((blk, LANES - nprim), F32)
        for p in range(per):
            comb[f, p * blk : (p + 1) * blk, :] = jnp.concatenate([parts[p], zero], axis=1)
        for p in range(half):
            both = jnp.concatenate([parts[p], parts[p + half]], axis=1)
            basis_out[f, p * blk : (p + 1) * blk, :] = both.astype(BF16)

        @pl.when(has[f])
        def _():
            basis_copy(f).start()

    for f in range(4):
        load_blocks[f].wait()
        for b in range(f * per, (f + 1) * per):
            left = jnp.concatenate([blocks[b, k] for k in range(knz)], axis=1)
            right = jnp.concatenate([weighted[pat_ref[b, k]] for k in range(knz)], axis=0)
            solved = wcol[b] * jnp.dot(left, right, preferred_element_type=F32)
            rows = slice(b * blk, (b + 1) * blk)
            acc[rows, :] = solved
            face_out[f, (b - f * per) * blk : (b - f * per + 1) * blk, :] = solved.astype(BF16)

        @pl.when(has[f])
        def _():
            face_copy(f).start()

    load_inv.wait()
    chunk = 512 if ncr <= 512 else LANES
    inv16 = inv[...].astype(BF16)

    def permute_columns(c, carry):
        at = pl.ds(pl.multiple_of(c * chunk, chunk), chunk)
        hit = lax.broadcasted_iota(jnp.int32, (ncr, chunk), 0) == ord_ref[:, at]
        inv_perm[:, at] = jnp.dot(
            inv16, jnp.where(hit, 1.0, 0.0).astype(BF16), preferred_element_type=F32
        ).astype(BF16)
        return carry

    lax.fori_loop(0, ncr // chunk, permute_columns, 0)

    wait_rows(gath, pv_s, pv_r)
    csol[own, :] = jnp.dot(
        inv_perm[...], gath[...], preferred_element_type=F32
    ).astype(BF16)
    send_rows(csol, cs_s, cs_r)

    wide = LANES // nprim
    lane = lax.broadcasted_iota(jnp.int32, (nprim, LANES), 1).astype(F32)
    for m, who in enumerate((j, jnp.maximum(j - 1, 0), jnp.minimum(j + 1, n_sy - 1))):
        at = pl.ds(pl.multiple_of((who // wide) * LANES, LANES), LANES)
        cols[m] = down_rows(ord_ref[:, at].astype(F32))
        col = cols[m, pl.ds(pl.multiple_of((who % wide) * nprim, nprim), nprim), :]
        for c in range(ncr // LANES):
            pick[m * nprim : (m + 1) * nprim, c * LANES : (c + 1) * LANES] = jnp.where(
                col == lane + float(c * LANES), 1.0, 0.0
            ).astype(BF16)

    wide_lane = lax.broadcasted_iota(jnp.int32, (LANES, face), 1).astype(F32)
    for f in range(4):
        for c in range(face // LANES):
            at = slice(c * LANES, (c + 1) * LANES)
            col = down_rows(sh_ref[f : f + 1, at].astype(F32))
            col = jnp.concatenate([col] * (face // LANES), axis=1)
            onehot[f, at, :] = jnp.where(col == wide_lane, 1.0, 0.0).astype(BF16)

    upper = lax.broadcasted_iota(jnp.int32, (face // 2, LANES), 1) >= nprim
    for f in range(4):

        @pl.when(has[f])
        def _():
            g = OPPOSITE[f]
            basis_copy(g).wait_recv()
            face_copy(g).wait_recv()

        packed = basis_in[f].astype(F32)
        first = jnp.concatenate(
            [jnp.zeros((face // 2, LANES - nprim), F32), packed[:, :nprim]], axis=1
        )
        second = jnp.where(upper, packed, 0.0)
        theirs = jnp.concatenate([first, second], axis=0).astype(BF16)
        moved = jnp.dot(
            onehot[f], jnp.concatenate([face_in[f], theirs], axis=1),
            preferred_element_type=F32,
        )
        rows = slice(f * face, (f + 1) * face)
        acc[rows, :] = acc[rows, :] + moved[:, :nvec]
        comb[f] = comb[f] + moved[:, nvec:]

    wait_rows(csol, cs_s, cs_r)
    taken = jnp.dot(pick[...], csol[...], preferred_element_type=F32).astype(BF16)
    for m in range(3):
        psol[m] = taken[m * nprim : (m + 1) * nprim, :]
    for f in (0, 1):

        @pl.when(has[f])
        def _():
            psol_copy(f).start()

    for f in (2, 3, 0, 1):
        if f < 2:

            @pl.when(has[f])
            def _():
                psol_copy(OPPOSITE[f]).wait_recv()

        other = psol_in[f] if f < 2 else psol[f - 1]
        both = jnp.concatenate([psol[0], other], axis=0)
        rows = slice(f * face, (f + 1) * face)
        out[rows, :] = (
            acc[rows, :]
            + jnp.dot(comb[f].astype(BF16), both, preferred_element_type=F32)
        ).astype(BF16)
        pltpu.make_async_copy(out.at[rows], out_hbm.at[rows], out_sem.at[f]).start()

    drain_rows(gath, pv_s, pv_r)
    drain_rows(csol, cs_s, cs_r)
    for f in range(4):

        @pl.when(has[f])
        def _():
            basis_copy(f).wait_send()
            face_copy(f).wait_send()
            if f < 2:
                psol_copy(f).wait_send()

        rows = slice(f * face, (f + 1) * face)
        pltpu.make_async_copy(out.at[rows], out_hbm.at[rows], out_sem.at[f]).wait()


def body(
    n_sx, n_sy,
    residual, weights, blocks, pattern, primal_basis, coarse_inverse, coarse_rows, shared_lists,
):
    ni, nvec = residual.shape[2:]
    nb, knz, blk = blocks.shape[2:5]
    nprim = primal_basis.shape[-1]
    ncr = coarse_rows.shape[-1]
    face = shared_lists.shape[-1]
    vmem, smem, hbm = (
        pl.BlockSpec(memory_space=space) for space in (pltpu.VMEM, pltpu.SMEM, pl.ANY)
    )
    dma = pltpu.SemaphoreType.DMA
    total = pl.pallas_call(
        functools.partial(kernel, n_sx, n_sy),
        out_shape=jax.ShapeDtypeStruct((ni, nvec), BF16),
        in_specs=[hbm, vmem, hbm, smem, hbm, hbm, vmem, vmem],
        out_specs=hbm,
        scratch_shapes=[
            pltpu.VMEM((ni, nvec), BF16),
            pltpu.VMEM((ni, nprim), BF16),
            pltpu.VMEM((nb, knz, blk, blk), BF16),
            pltpu.VMEM((nprim, ncr), F32),
            pltpu.VMEM((nb, blk, LANES), F32),
            pltpu.VMEM((nb, blk, nvec), BF16),
            pltpu.VMEM((ni, nvec), F32),
            pltpu.VMEM((4, face, LANES), F32),
            pltpu.VMEM((4, face, face), BF16),
            pltpu.VMEM((nprim, ncr), BF16),
            pltpu.VMEM((3 * nprim, ncr), BF16),
            pltpu.VMEM((3, LANES, LANES), F32),
            pltpu.VMEM((ncr, nvec), BF16),
            pltpu.VMEM((ncr, nvec), BF16),
            pltpu.VMEM((3, nprim, nvec), BF16),
            pltpu.VMEM((4, face, nvec), BF16),
            pltpu.VMEM((4, face // 2, LANES), BF16),
            pltpu.VMEM((4, face, nvec), BF16),
            pltpu.VMEM((4, face // 2, LANES), BF16),
            pltpu.VMEM((2, nprim, nvec), BF16),
            pltpu.VMEM((ni, nvec), BF16),
            dma((3,)), dma((4,)), dma((4,)),
            dma((n_sy,)), dma((n_sy,)), dma((n_sy,)), dma((n_sy,)),
            dma((4,)), dma((4,)), dma((4,)), dma((4,)), dma((2,)), dma((2,)),
        ],
        compiler_params=pltpu.CompilerParams(
            collective_id=0, has_side_effects=True, vmem_limit_bytes=40 * 1024 * 1024
        ),
    )(
        residual[0, 0], weights[0], blocks[0, 0], pattern[0, 0], primal_basis[0, 0],
        coarse_inverse[0], coarse_rows, shared_lists[0, 0],
    )
    return total[None, None]


def solution(mesh):
    return jax.shard_map(
        functools.partial(body, mesh.shape["sx"], mesh.shape["sy"]),
        mesh=mesh,
        in_specs=(
            P("sx", "sy", None, None),
            P("sx", "sy", None),
            P("sx", "sy", None, None, None, None),
            P("sx", "sy", None, None),
            P("sx", "sy", None, None),
            P("sx", "sy", None),
            P("sx", None),
            P("sx", "sy", None, None),
        ),
        out_specs=P("sx", "sy", None, None),
        check_vma=False,
    )
```

time: 71.7 us -> 26.8 us (0.37)
  blocking collectives: 20.9 us -> 0 us
  Pallas kernels: 0 us -> 18 us
  local copies, waits for them, and re-layouts: 21.1 us -> 8.38 us
  starting transfers between devices: 10.2 us -> 0 us
  other arithmetic: 6.74 us -> 0 us
  waiting for transfers between devices: 6.46 us -> 0 us
  matrix products: 5.47 us -> 0 us
    all_gather x2 -> x0, blocking collectives: 20.9 us -> none  [the longest x1 11.8 us: body(): gathered = lax.all_gather(primal_vals, 'sy', axis=0, tiled=True)]
    pallas_call x0 -> x1, Pallas kernels: none -> 18 us  [body(): pl.pallas_call(functools.partial(kernel, n_sx, n_sy), out_shape=jax.Shape...]
    ppermute x4 -> x0, starting transfers between devices: 10.2 us -> none  [the longest x2 7.61 us: with_halo(): lax.ppermute(lax.slice_in_dim(block, block.shape[dim] - width, None, axis...]
    gather x6 -> x0, local copies, waits for them, and re-layouts: 8.77 us -> none  [the longest x1 2.15 us: body(): pieces = weighted.reshape(nblocks, blk, nvec)[pattern[0, 0]]]
    unnamed x18 -> x14, local copies, waits for them, and re-layouts: 1.02 us -> 7.62 us
    ppermute x4 -> x0, waiting for transfers between devices: 6.46 us -> none  [the longest x2 4.59 us: with_halo(): lax.ppermute(lax.slice_in_dim(block, 0, width, axis=dim), axis, backward)]
    dot_general x4 -> x0, matrix products: 5.47 us -> none  [the longest x1 2.28 us: body(): jnp.einsum('bkrc,bkcn->brn', blocks[0, 0], pieces, preferred_element_type...]
    convert_element_type x2 -> x0, other arithmetic: 3.52 us -> none  [the longest x1 2.12 us: body(): return total.reshape(1, 1, ninter, nvec).astype(jnp.bfloat16)]
  transfers between devices with their start and end apart: 4 -> 0, of which waited for: 2 -> 0; matrix products, arithmetic and copies ran while one was open for 4% -> 0% of each run, Pallas kernels for 0% -> 0%
where the time goes in v1:
time: 26.8 us; the launch traced here: 26.4 us
  Pallas kernels  18 us (67%)
  local copies, waits for them, and re-layouts  8.38 us (31%)
    pallas_call x1, Pallas kernels, body(): pl.pallas_call(functools.partial(kernel, n_sx, n_sy), out_shape=jax.Shape...  18 us
    unnamed x14, local copies, waits for them, and re-layouts  7.62 us
    squeeze x1, local copies, waits for them, and re-layouts, body(): pattern[0, 0]  0.76 us

profile of v1, /device:TPU:0, one launch (start us, length us, event | category | flops | bytes accessed | tf_op | source)
XLA Modules:
  0.0 26.4 jit_solution(6471565055271250355)
XLA Ops:
  0.0 0.8 %copy.10.pat_ref = s32[16,4]{1,0:T(8,128)S(1)} copy(s32[16,4]{0,1:T(4,128)} %bitcast.15) | data formatting | bytes 512 | tf_op jit(solution)/shard_map/squeeze | solution.py:329
  0.8 1.2 %copy.9 = bf16[1,1,2048,64]{3,2,1,0:T(8,128)(2,1)S(1)} copy(bf16[1,1,2048,64]{2,3,1,0:T(8,128)(2,1)} %param.12) | data formatting | bytes 524288 | tf_op args[4]
  2.0 0.0 copy-start
  2.0 1.6 %copy-done = bf16[1,1,16,4,128,128]{5,4,3,2,1,0:T(8,128)(2,1)S(1)} copy-done((bf16[1,1,16,4,128,128]{5,4,3,2,1,0:T(8,128)(2,1)S(1)}, bf16[1,1,16,4,128,128]{5,4,3,2,1,0:T(8,128)(2,1)}, u32[]{:S(2)}) %copy-start) | copy-done | bytes 2097176
  3.6 0.0 copy-start.1
  3.6 1.0 %copy-done.1 = bf16[1,1,2048,128]{3,2,1,0:T(8,128)(2,1)S(1)} copy-done((bf16[1,1,2048,128]{3,2,1,0:T(8,128)(2,1)S(1)}, bf16[1,1,2048,128]{3,2,1,0:T(8,128)(2,1)}, u32[]{:S(2)}) %copy-start.1) | copy-done | bytes 524312
  4.6 0.0 copy-start.2
  4.6 0.9 %copy-done.2 = f32[1,64,512]{2,1,0:T(8,128)S(1)} copy-done((f32[1,64,512]{2,1,0:T(8,128)S(1)}, f32[1,64,512]{2,1,0:T(8,128)}, u32[]{:S(2)}) %copy-start.2) | copy-done | bytes 131096
  5.5 0.0 copy-start.3
  5.5 0.7 %copy-done.3 = f32[1,1,2048]{2,1,0:T(1,128)S(1)} copy-done((f32[1,1,2048]{2,1,0:T(1,128)S(1)}, f32[1,1,2048]{2,1,0:T(1,128)}, u32[]{:S(2)}) %copy-start.3) | copy-done | bytes 8216
  6.2 0.0 copy-start.4
  6.2 0.7 %copy-done.4 = s32[1,1,4,512]{3,2,1,0:T(4,128)S(1)} copy-done((s32[1,1,4,512]{3,2,1,0:T(4,128)S(1)}, s32[1,1,4,512]{3,2,1,0:T(4,128)}, u32[]{:S(2)}) %copy-start.4) | copy-done | bytes 8216
  6.9 0.0 copy-start.5
  6.9 0.7 %copy-done.5 = s32[1,512]{1,0:T(1,128)S(1)} copy-done((s32[1,512]{1,0:T(1,128)S(1)}, s32[1,512]{1,0:T(1,128)}, u32[]{:S(2)}) %copy-start.5) | copy-done | bytes 2072
  7.6 18.0 %shard_map.82 = bf16[2048,128]{1,0:T(8,128)(2,1)S(1)} custom-call(bf16[2048,128]{1,0:T(8,128)(2,1)S(1)} %bitcast.11, f32[1,2048]{1,0:T(1,128)S(1)} %bitcast.13, bf16[16,4,128,128]{3,2,1,0:T(8,128)(2,1)S(1)} %bitcast.8, s32[16,4]{1,0:T(8,128)S(1)} %copy.10.pat_ref, bf16[2048,64]{1,0:T(8,128)(2,1)S(1)} %bitcast.10, f32[64,512]{1,0:T(8,128)S(1)} %bitcast.12, ...), custom_call_target="tpu_custom_call" | custom-call | tf_op jit(solution)/shard_map/pallas_call | solution.py:294
  25.6 0.8 %copy.12 = bf16[1,1,2048,128]{3,2,1,0:T(8,128)(2,1)} copy(bf16[1,1,2048,128]{3,2,1,0:T(8,128)(2,1)S(1)} %bitcast.9) | data formatting | bytes 1048576
Async XLA Ops:
  2.0 1.6 %copy-start = (bf16[1,1,16,4,128,128]{5,4,3,2,1,0:T(8,128)(2,1)S(1)}, bf16[1,1,16,4,128,128]{5,4,3,2,1,0:T(8,128)(2,1)}, u32[]{:S(2)}) copy-start(bf16[1,1,16,4,128,128]{5,4,3,2,1,0:T(8,128)(2,1)} %param.10) | copy-start | bytes 6291460
  3.6 1.0 %copy-start.1 = (bf16[1,1,2048,128]{3,2,1,0:T(8,128)(2,1)S(1)}, bf16[1,1,2048,128]{3,2,1,0:T(8,128)(2,1)}, u32[]{:S(2)}) copy-start(bf16[1,1,2048,128]{3,2,1,0:T(8,128)(2,1)} %param.8) | copy-start | bytes 1572868
  4.6 0.9 %copy-start.2 = (f32[1,64,512]{2,1,0:T(8,128)S(1)}, f32[1,64,512]{2,1,0:T(8,128)}, u32[]{:S(2)}) copy-start(f32[1,64,512]{2,1,0:T(8,128)} %param.13) | copy-start | bytes 393220
  5.5 0.7 %copy-start.3 = (f32[1,1,2048]{2,1,0:T(1,128)S(1)}, f32[1,1,2048]{2,1,0:T(1,128)}, u32[]{:S(2)}) copy-start(f32[1,1,2048]{2,1,0:T(1,128)} %param.9) | copy-start | bytes 24580
  6.2 0.7 %copy-start.4 = (s32[1,1,4,512]{3,2,1,0:T(4,128)S(1)}, s32[1,1,4,512]{3,2,1,0:T(4,128)}, u32[]{:S(2)}) copy-start(s32[1,1,4,512]{3,2,1,0:T(4,128)} %param.15) | copy-start | bytes 24580
  6.9 0.7 %copy-start.5 = (s32[1,512]{1,0:T(1,128)S(1)}, s32[1,512]{1,0:T(1,128)}, u32[]{:S(2)}) copy-start(s32[1,512]{1,0:T(1,128)} %ord_ref.1) | copy-start | bytes 6148

commit v2 on v1

--- a/solution.py
+++ b/solution.py
@@ -20,9 +20,10 @@
 
 def kernel(
     n_sx, n_sy,
-    res_hbm, w_ref, blocks_hbm, pat_ref, basis_hbm, inv_hbm, ord_ref, sh_ref,
+    res_hbm, w_hbm, blocks_hbm, pat_hbm, basis_hbm, inv_hbm, ord_hbm, sh_hbm,
     out_hbm,
-    res, basis, blocks, inv, wcol, weighted, acc, comb, onehot, inv_perm, pick, cols,
+    res, w_ref, basis, blocks, inv, ord_ref, sh_ref, pat_ref,
+    wcol, weighted, acc, comb, onehot, inv_perm, pick, cols,
     gath, csol, psol, face_out, basis_out, face_in, basis_in, psol_in, out,
     in_sem, blk_sem, out_sem, pv_s, pv_r, cs_s, cs_r, fb_s, fb_r, fw_s, fw_r, ps_s, ps_r,
 ):
@@ -33,19 +34,23 @@
     face = ni // 4
     per = face // blk
 
-    load_basis = pltpu.make_async_copy(basis_hbm, basis, in_sem.at[0])
-    load_res = pltpu.make_async_copy(res_hbm, res, in_sem.at[1])
-    load_inv = pltpu.make_async_copy(inv_hbm, inv, in_sem.at[2])
+    loads = [
+        pltpu.make_async_copy(source, target, in_sem.at[n])
+        for n, (source, target) in enumerate(
+            (
+                (w_hbm, w_ref), (basis_hbm, basis), (res_hbm, res), (ord_hbm, ord_ref),
+                (sh_hbm, sh_ref), (pat_hbm, pat_ref), (inv_hbm, inv),
+            )
+        )
+    ]
+    load_w, load_basis, load_res, load_ord, load_sh, load_pat, load_inv = loads
     load_blocks = [
         pltpu.make_async_copy(
             blocks_hbm.at[pl.ds(f * per, per)], blocks.at[pl.ds(f * per, per)], blk_sem.at[f]
         )
         for f in range(4)
     ]
-    load_basis.start()
-    load_res.start()
-    load_inv.start()
-    for copy in load_blocks:
+    for copy in loads + load_blocks:
         copy.start()
 
     has = (i > 0, i < n_sx - 1, j > 0, j < n_sy - 1)
@@ -125,17 +130,17 @@
             if f < 2:
                 psol_in[f] = jnp.zeros(psol_in.shape[1:], BF16)
 
-    for b in range(nb):
-        wcol[b] = down_rows(w_ref[0:1, b * blk : (b + 1) * blk])
+    load_w.wait()
     load_basis.wait()
+    for f in range(4):
+        at = slice(f * face, (f + 1) * face)
+        basis_out[f] = (w_ref[0:1, at] * basis[:, at].astype(F32)).astype(BF16)
     load_res.wait()
-    for b in range(nb):
-        rows = slice(b * blk, (b + 1) * blk)
-        weighted[b] = (wcol[b] * res[rows, :].astype(F32)).astype(BF16)
-    pv = lax.dot_general(
-        basis[...], weighted[...].reshape(ni, nvec), (((0,), (0,)), ((), ())),
-        preferred_element_type=F32,
-    )
+    pv = jnp.zeros((nprim, nvec), F32)
+    for f in range(4):
+        pv += jnp.dot(
+            basis_out[f], res[f * face : (f + 1) * face, :], preferred_element_type=F32
+        )
     own = pl.ds(pl.multiple_of(j * nprim, nprim), nprim)
     gath[own, :] = pv.astype(BF16)
 
@@ -143,29 +148,23 @@
         barrier, n_sy - 1 + has[0].astype(jnp.int32) + has[1].astype(jnp.int32)
     )
     send_rows(gath, pv_s, pv_r)
-
-    half = per // 2
-    for f in range(4):
-        parts = []
-        for b in range(f * per, (f + 1) * per):
-            rows = slice(b * blk, (b + 1) * blk)
-            parts.append(wcol[b][:, :nprim] * basis[rows, :].astype(F32))
-        zero = jnp.zeros((blk, LANES - nprim), F32)
-        for p in range(per):
-            comb[f, p * blk : (p + 1) * blk, :] = jnp.concatenate([parts[p], zero], axis=1)
-        for p in range(half):
-            both = jnp.concatenate([parts[p], parts[p + half]], axis=1)
-            basis_out[f, p * blk : (p + 1) * blk, :] = both.astype(BF16)
+    for f in range(4):
 
         @pl.when(has[f])
         def _():
             basis_copy(f).start()
 
+    for b in range(nb):
+        rows = slice(b * blk, (b + 1) * blk)
+        wcol[b] = down_rows(w_ref[0:1, rows])
+        weighted[b] = (wcol[b] * res[rows, :].astype(F32)).astype(BF16)
+
+    load_pat.wait()
     for f in range(4):
         load_blocks[f].wait()
         for b in range(f * per, (f + 1) * per):
             left = jnp.concatenate([blocks[b, k] for k in range(knz)], axis=1)
-            right = jnp.concatenate([weighted[pat_ref[b, k]] for k in range(knz)], axis=0)
+            right = jnp.concatenate([weighted[pat_ref[k, b]] for k in range(knz)], axis=0)
             solved = wcol[b] * jnp.dot(left, right, preferred_element_type=F32)
             rows = slice(b * blk, (b + 1) * blk)
             acc[rows, :] = solved
@@ -176,6 +175,8 @@
             face_copy(f).start()
 
     load_inv.wait()
+    load_ord.wait()
+    load_sh.wait()
     chunk = 512 if ncr <= 512 else LANES
     inv16 = inv[...].astype(BF16)
 
@@ -214,7 +215,6 @@
             col = jnp.concatenate([col] * (face // LANES), axis=1)
             onehot[f, at, :] = jnp.where(col == wide_lane, 1.0, 0.0).astype(BF16)
 
-    upper = lax.broadcasted_iota(jnp.int32, (face // 2, LANES), 1) >= nprim
     for f in range(4):
 
         @pl.when(has[f])
@@ -223,19 +223,15 @@
             basis_copy(g).wait_recv()
             face_copy(g).wait_recv()
 
-        packed = basis_in[f].astype(F32)
-        first = jnp.concatenate(
-            [jnp.zeros((face // 2, LANES - nprim), F32), packed[:, :nprim]], axis=1
-        )
-        second = jnp.where(upper, packed, 0.0)
-        theirs = jnp.concatenate([first, second], axis=0).astype(BF16)
-        moved = jnp.dot(
-            onehot[f], jnp.concatenate([face_in[f], theirs], axis=1),
-            preferred_element_type=F32,
-        )
         rows = slice(f * face, (f + 1) * face)
-        acc[rows, :] = acc[rows, :] + moved[:, :nvec]
-        comb[f] = comb[f] + moved[:, nvec:]
+        acc[rows, :] = acc[rows, :] + jnp.dot(
+            onehot[f], face_in[f], preferred_element_type=F32
+        )
+        moved = lax.dot_general(
+            basis_in[f], onehot[f], (((1,), (1,)), ((), ())), preferred_element_type=F32
+        )
+        both = jnp.concatenate([basis_out[f].astype(F32), moved], axis=0)
+        comb[f] = both.T.astype(BF16)
 
     wait_rows(csol, cs_s, cs_r)
     taken = jnp.dot(pick[...], csol[...], preferred_element_type=F32).astype(BF16)
@@ -259,7 +255,7 @@
         rows = slice(f * face, (f + 1) * face)
         out[rows, :] = (
             acc[rows, :]
-            + jnp.dot(comb[f].astype(BF16), both, preferred_element_type=F32)
+            + jnp.dot(comb[f], both, preferred_element_type=F32)
         ).astype(BF16)
         pltpu.make_async_copy(out.at[rows], out_hbm.at[rows], out_sem.at[f]).start()
 
@@ -287,24 +283,26 @@
     nprim = primal_basis.shape[-1]
     ncr = coarse_rows.shape[-1]
     face = shared_lists.shape[-1]
-    vmem, smem, hbm = (
-        pl.BlockSpec(memory_space=space) for space in (pltpu.VMEM, pltpu.SMEM, pl.ANY)
-    )
+    hbm = pl.BlockSpec(memory_space=pltpu.HBM)
     dma = pltpu.SemaphoreType.DMA
     total = pl.pallas_call(
         functools.partial(kernel, n_sx, n_sy),
         out_shape=jax.ShapeDtypeStruct((ni, nvec), BF16),
-        in_specs=[hbm, vmem, hbm, smem, hbm, hbm, vmem, vmem],
+        in_specs=[hbm] * 8,
         out_specs=hbm,
         scratch_shapes=[
             pltpu.VMEM((ni, nvec), BF16),
-            pltpu.VMEM((ni, nprim), BF16),
+            pltpu.VMEM((1, ni), F32),
+            pltpu.VMEM((nprim, ni), BF16),
             pltpu.VMEM((nb, knz, blk, blk), BF16),
             pltpu.VMEM((nprim, ncr), F32),
+            pltpu.VMEM((1, ncr), jnp.int32),
+            pltpu.VMEM((4, face), jnp.int32),
+            pltpu.SMEM((knz, nb), jnp.int32),
             pltpu.VMEM((nb, blk, LANES), F32),
             pltpu.VMEM((nb, blk, nvec), BF16),
             pltpu.VMEM((ni, nvec), F32),
-            pltpu.VMEM((4, face, LANES), F32),
+            pltpu.VMEM((4, face, 2 * nprim), BF16),
             pltpu.VMEM((4, face, face), BF16),
             pltpu.VMEM((nprim, ncr), BF16),
             pltpu.VMEM((3 * nprim, ncr), BF16),
@@ -313,20 +311,20 @@
             pltpu.VMEM((ncr, nvec), BF16),
             pltpu.VMEM((3, nprim, nvec), BF16),
             pltpu.VMEM((4, face, nvec), BF16),
-            pltpu.VMEM((4, face // 2, LANES), BF16),
+            pltpu.VMEM((4, nprim, face), BF16),
             pltpu.VMEM((4, face, nvec), BF16),
-            pltpu.VMEM((4, face // 2, LANES), BF16),
+            pltpu.VMEM((4, nprim, face), BF16),
             pltpu.VMEM((2, nprim, nvec), BF16),
             pltpu.VMEM((ni, nvec), BF16),
-            dma((3,)), dma((4,)), dma((4,)),
+            dma((7,)), dma((4,)), dma((4,)),
             dma((n_sy,)), dma((n_sy,)), dma((n_sy,)), dma((n_sy,)),
             dma((4,)), dma((4,)), dma((4,)), dma((4,)), dma((2,)), dma((2,)),
         ],
         compiler_params=pltpu.CompilerParams(
-            collective_id=0, has_side_effects=True, vmem_limit_bytes=40 * 1024 * 1024
+            collective_id=0, has_side_effects=True, vmem_limit_bytes=64 * 1024 * 1024
         ),
     )(
-        residual[0, 0], weights[0], blocks[0, 0], pattern[0, 0], primal_basis[0, 0],
+        residual[0, 0], weights[0], blocks[0, 0], pattern[0, 0].T, primal_basis[0, 0].T,
         coarse_inverse[0], coarse_rows, shared_lists[0, 0],
     )
     return total[None, None]

time: 26.8 us -> 19.4 us (0.72)
  local copies, waits for them, and re-layouts: 8.38 us -> 1.87 us
  Pallas kernels: 18 us -> 17.3 us
    unnamed x14 -> x1, local copies, waits for them, and re-layouts: 7.62 us -> 1.87 us
    squeeze x1 -> x0, local copies, waits for them, and re-layouts: 0.76 us -> none  [body(): pattern[0, 0]]
    pallas_call x1, Pallas kernels: 18 us -> 17.3 us  [body(): pl.pallas_call(functools.partial(kernel, n_sx, n_sy), out_shape=jax.Shape...]
where the time goes in v2:
time: 19.4 us; the launch traced here: 19.2 us
  Pallas kernels  17.3 us (89%)
  local copies, waits for them, and re-layouts  1.87 us (10%)
    pallas_call x1, Pallas kernels, body(): pl.pallas_call(functools.partial(kernel, n_sx, n_sy), out_shape=jax.Shape...  17.3 us
    unnamed x1, local copies, waits for them, and re-layouts  1.87 us

profile of v2, /device:TPU:0, one launch (start us, length us, event | category | flops | bytes accessed | tf_op | source)
XLA Modules:
  0.0 19.2 jit_solution(12850152471192046255)
XLA Ops:
  0.0 17.3 %shard_map.82 = bf16[2048,128]{1,0:T(8,128)(2,1)} custom-call(bf16[2048,128]{1,0:T(8,128)(2,1)} %bitcast.14, f32[1,2048]{1,0:T(1,128)} %bitcast.17, bf16[16,4,128,128]{3,2,1,0:T(8,128)(2,1)} %bitcast.12, s32[4,16]{1,0:T(4,128)} %bitcast.19, bf16[64,2048]{1,0:T(8,128)(2,1)} %bitcast.15, f32[64,512]{1,0:T(8,128)} %bitcast.16, s32[1,512]{1,0:T(1,128)} %ord_hbm.1, ...), custom_call_target="tpu_custom_call" | custom-call | tf_op jit(solution)/shard_map/pallas_call | solution.py:288
  17.3 1.9 %copy.10 = bf16[1,1,2048,128]{3,2,1,0:T(8,128)(2,1)} copy(bf16[1,1,2048,128]{3,2,1,0:T(8,128)(2,1)} %bitcast.13) | data formatting | bytes 1048576
